TPU v7x, 32 devices: a whole 2x2x4 slice. The times are simulated.
32 devices in a mesh: expert: 8 (over z, x), width: 4 (over y, core).
Axes of the slice: x: 2, y: 2, z: 4, core: 2. Of those that a mesh axis runs over, the one named last changes fastest.
Arguments:
- tokens: bfloat16 [1024, 4096], P('expert'), may hold values from -6 to 6
- expert_ids: int32 [1024, 8], P('expert'), may hold values from 0 to 15, all different within a row; in each aligned block of 128 rows (0 to 127, 128 to 255, ...) at most 128 rows name the same one
- combine_weights: float32 [1024, 8], P('expert'), may hold values from 0.05 to 0.3
- gate_weight: bfloat16 [16, 4096, 1536], P('expert', None, 'width'), may hold values from -0.09375 to 0.09375
- up_weight: bfloat16 [16, 4096, 1536], P('expert', None, 'width'), may hold values from -0.09375 to 0.09375
- down_weight: bfloat16 [16, 1536, 4096], P('expert', 'width'), may hold values from -0.15625 to 0.15625
Outputs:
- mixed: bfloat16 [1024, 4096], P('expert', 'width')
Inputs may be any that keep to these rules, and one draw needn't show every extreme that they name: `expert_ids`: each token names 8 different experts. Within the tokens of one index of expert (aligned blocks of 128 tokens) no expert is named by more than 128 tokens, a bound that some block reaches.
All inputs are finite; a program needn't handle non-finite values.
Results may differ from a plain program's by a relative error of at most 0.012.
Values may be sent and summed in bfloat16 or wider, within the bound.
A program may use at most 128 MiB of HBM per device.

v0:
```python
import jax
import jax.numpy as jnp
from jax import lax
from jax.sharding import PartitionSpec as P


def local(tokens, expert_ids, combine_weights, gate_weight, up_weight, down_weight):
    tok_rows = tokens.shape[0]
    top_count = expert_ids.shape[1]
    exp_local = gate_weight.shape[0]
    n_expert = lax.axis_size("expert")
    n_width = lax.axis_size("width")
    experts_all = exp_local * n_expert
    slots = 2 * tok_rows * top_count // experts_all
    width_all = tokens.shape[1]
    cols = width_all // n_width
    flat_ids = expert_ids.reshape(-1)
    onehot = (flat_ids[:, None] == jnp.arange(experts_all, dtype=jnp.int32)[None, :]).astype(
        jnp.int32
    )
    rank = jnp.sum(jnp.cumsum(onehot, axis=0) * onehot, axis=1) - 1
    slot = flat_ids * slots + rank
    token_index = jnp.arange(tok_rows * top_count, dtype=jnp.int32) // top_count
    table = jnp.full((experts_all * slots,), tok_rows, jnp.int32).at[slot].set(token_index)
    padded = jnp.concatenate([tokens, jnp.zeros((1, width_all), jnp.bfloat16)], axis=0)
    outgoing = padded[table].reshape(n_expert, exp_local, slots, width_all)
    own_cols = lax.dynamic_slice_in_dim(outgoing, lax.axis_index("width") * cols, cols, 3)
    arrived_cols = lax.all_to_all(own_cols, "expert", split_axis=0, concat_axis=0, tiled=True)
    arrived = lax.all_gather(arrived_cols, "width", axis=3, tiled=True)
    gate = jnp.einsum("skmd,kdf->skmf", arrived, gate_weight, preferred_element_type=jnp.float32)
    up_part = jnp.einsum("skmd,kdf->skmf", arrived, up_weight, preferred_element_type=jnp.float32)
    hidden = (jax.nn.silu(gate) * up_part).astype(jnp.bfloat16)
    partial_value = jnp.einsum(
        "skmf,kfd->skmd", hidden, down_weight, preferred_element_type=jnp.float32
    )
    reduced = lax.psum_scatter(
        partial_value.astype(jnp.bfloat16), "width", scatter_dimension=3, tiled=True
    ).astype(jnp.float32)
    returned = lax.all_to_all(
        reduced.astype(jnp.bfloat16), "expert", split_axis=0, concat_axis=0, tiled=True
    ).astype(reduced.dtype)
    picked = returned.reshape(experts_all * slots, cols)[slot].reshape(tok_rows, top_count, cols)
    mixed = jnp.sum(combine_weights[:, :, None] * picked, axis=1)
    return mixed.astype(jnp.bfloat16)


def solution(mesh):
    placed = (
        P("expert", None),
        P("expert", None),
        P("expert", None),
        P("expert", None, "width"),
        P("expert", None, "width"),
        P("expert", "width", None),
    )
    return jax.shard_map(
        local, mesh=mesh, in_specs=placed, out_specs=P("expert", "width"), check_vma=False
    )
```

profile of v0, /device:TPU:0, one launch (start us, length us, event | category | flops | bytes accessed | tf_op | source)
XLA Modules:
  0.0 540.2 jit_solution(17724048829518535215)
XLA Ops:
  6.5 0.0 all-gather.2.cloned.1.call-start
  6.5 0.8 copy.20
  7.3 0.1 eq.29
  7.4 0.1 eq.25
  7.5 0.7 broadcast_multiply_fusion
  8.2 4.5 reduce-window.6
  12.7 0.1 slice.12
  12.8 0.1 copy.22
  13.0 0.1 copy.23
  13.1 0.1 broadcast_add_fusion
  13.2 0.1 copy.19
  13.3 0.1 mul.40
  13.4 4.3 scatter_custom_fusion
  17.7 1.3 concatenate.3
  19.1 14.3 %gather_fusion = bf16[2048,4096]{1,0:T(8,128)(2,1)} fusion(bf16[129,4096]{1,0:T(8,128)(2,1)S(1)} %concatenate.3, s32[2048]{0:T(1024)S(1)} %fusion.15), kind=kCustom, calls=%fused_computation | custom fusion | bytes 33562624 | tf_op jit(solution)/shard_map/gather | solution.py:26
  33.4 2.6 constant_dynamic-slice_fusion
  36.0 100.3 %all_to_all.10 = bf16[8,2,128,1024]{3,2,1,0:T(8,128)(2,1)S(1)} all-to-all(bf16[8,2,128,1024]{3,2,1,0:T(8,128)(2,1)S(1)} %constant_dynamic-slice_fusion), channel_id=1, replica_groups=mesh['expert'=8,'width'=4] {'expert'}, dimensions={0} | all-to-all | bytes 8388608 | tf_op jit(solution)/shard_map/all_to_all | solution.py:28
  136.3 2.4 copy.24
  138.6 0.0 all-gather.2.cloned.1.call-update
  138.7 0.2 reduce-scatter.2.cloned.1.call-start
  138.9 104.9 %all-gather.2.cloned.1.call-done = bf16[8,2,128,4096]{3,2,0,1:T(8,128)(2,1)} async-done(((bf16[8,2,128,1024]{3,2,0,1:T(8,128)(2,1)}), bf16[8,2,128,4096]{3,2,0,1:T(8,128)(2,1)}) %all-gather.2.cloned.1.call-update) | async-done | bytes 16777232 | tf_op jit(solution)/shard_map/all_gather | solution.py:29
  243.8 0.0 copy-start.1
  243.8 14.1 %fusion.1 = f32[2,8,128,384]{3,2,1,0:T(8,128)S(1)} fusion(bf16[8,2,128,4096]{3,2,0,1:T(8,128)(2,1)} %all-gather.2.cloned.1.call-done, bf16[2,4096,384]{2,1,0:T(8,128)(2,1)} %param.10), kind=kOutput, calls=%fused_computation.5 | convolution fusion | flops 6442450944 | bytes 26214400 | tf_op jit(solution)/shard_map/skmd,kdf->skmf/dot_general | solution.py:31
  257.9 0.0 copy-done.1
  257.9 11.2 %fusion.6 = bf16[8,2,128,384]{3,2,0,1:T(8,128)(2,1)S(1)} fusion(f32[2,8,128,384]{3,2,1,0:T(8,128)S(1)} %fusion.1, bf16[8,2,128,4096]{3,2,0,1:T(8,128)(2,1)S(1)} %copy-done.1, bf16[2,4096,384]{2,1,0:T(8,128)(2,1)} %param.9), kind=kOutput, calls=%fused_computation.13 | convolution fusion | flops 6447169536 | bytes 27787264 | tf_op jit(solution)/shard_map/skmd,kdf->skmf/dot_general | solution.py:30
  269.2 15.2 %convert_bitcast_fusion = bf16[8,2,128,4096]{3,2,0,1:T(8,128)(2,1)} fusion(bf16[8,2,128,384]{3,2,0,1:T(8,128)(2,1)S(1)} %fusion.6, bf16[2,384,4096]{2,1,0:T(8,128)(2,1)} %param.11), kind=kOutput, calls=%fused_computation.3 | convolution fusion | flops 6450839552 | bytes 24641536 | tf_op jit(solution)/shard_map/skmf,kfd->skmd/dot_general | solution.py:33
  284.3 0.0 reduce-scatter.2.cloned.1.call-update
  284.3 125.0 %reduce-scatter.2.cloned.1.call-done = bf16[8,2,128,1024]{3,2,0,1:T(8,128)(2,1)} async-done(((bf16[8,2,128,4096]{3,2,0,1:T(8,128)(2,1)}), bf16[8,2,128,1024]{3,2,0,1:T(8,128)(2,1)}) %reduce-scatter.2.cloned.1.call-update) | async-done | bytes 4194320 | tf_op jit(solution)/shard_map/reduce_scatter | solution.py:36
  409.4 4.7 copy.25
  414.1 0.0 copy-start
  414.1 5.6 %all-to-all-start.1 = ((bf16[8,2,128,1024]{3,2,1,0:T(8,128)(2,1)}), bf16[8,2,128,1024]{3,2,1,0:T(8,128)(2,1)}, u32[]{:S(2)}, u32[]{:S(2)}) async-start(bf16[8,2,128,1024]{3,2,1,0:T(8,128)(2,1)} %copy.25), calls=%async_computation.2 | async-start | bytes 8388608 | tf_op jit(solution)/shard_map/all_to_all | solution.py:39
  419.8 0.0 copy-done
  419.8 0.1 copy.18
  419.9 93.0 %all-to-all-done.1 = bf16[8,2,128,1024]{3,2,1,0:T(8,128)(2,1)} async-done(((bf16[8,2,128,1024]{3,2,1,0:T(8,128)(2,1)}), bf16[8,2,128,1024]{3,2,1,0:T(8,128)(2,1)}, u32[]{:S(2)}, u32[]{:S(2)}) %all-to-all-start.1) | async-done | bytes 4194336 | tf_op jit(solution)/shard_map/all_to_all | solution.py:39
  512.9 6.5 %bitcast_convert_fusion = f32[2048,1024]{1,0:T(8,128)} fusion(bf16[8,2,128,1024]{3,2,1,0:T(8,128)(2,1)} %all-to-all-done.1), kind=kLoop, calls=%fused_computation.9 | loop fusion | flops 2097152 | bytes 12582912 | tf_op jit(solution)/shard_map/reshape | solution.py:42
  519.3 9.8 %gather_fusion.1 = f32[1024,1024]{1,0:T(8,128)} fusion(f32[2048,1024]{1,0:T(8,128)} %bitcast_convert_fusion, s32[1024]{0:T(1024)S(1)} %broadcast_clamp_fusion), kind=kCustom, calls=%fused_computation.1 | custom fusion | bytes 8392704 | tf_op jit(solution)/shard_map/gather | solution.py:42
  529.2 4.2 fusion.5
  (9 shorter events, 0.1 us)
Async XLA Ops:
  6.5 237.2 %all-gather.2.cloned.1.call-start = ((), (), s32[]{:S(2)}) async-start(), calls=%async_computation.3 | async-start | bytes 20971520 | tf_op jit(solution)/shard_map/all_gather | solution.py:29
  138.7 270.7 %reduce-scatter.2.cloned.1.call-start = ((), (), s32[]{:S(2)}) async-start(), calls=%async_computation.4 | async-start | bytes 20971520 | tf_op jit(solution)/shard_map/reduce_scatter | solution.py:36
  243.8 14.1 %copy-start.1 = (bf16[8,2,128,4096]{3,2,0,1:T(8,128)(2,1)S(1)}, bf16[8,2,128,4096]{3,2,0,1:T(8,128)(2,1)}, u32[]{:S(2)}) copy-start(bf16[8,2,128,4096]{3,2,0,1:T(8,128)(2,1)} %all-gather.2.cloned.1.call-done) | copy-start | bytes 50331652
  414.1 5.6 %copy-start = (f32[128,8]{0,1:T(8,128)S(1)}, f32[128,8]{0,1:T(8,128)}, u32[]{:S(2)}) copy-start(f32[128,8]{0,1:T(8,128)} %param.8) | copy-start | bytes 12292
  414.1 98.8 %all-to-all-start.1 = ((bf16[8,2,128,1024]{3,2,1,0:T(8,128)(2,1)}), bf16[8,2,128,1024]{3,2,1,0:T(8,128)(2,1)}, u32[]{:S(2)}, u32[]{:S(2)}) async-start(bf16[8,2,128,1024]{3,2,1,0:T(8,128)(2,1)} %copy.25), calls=%async_computation.2 | async-start | bytes 8388608 | tf_op jit(solution)/shard_map/all_to_all | solution.py:39
Sparse Core Ops, SparseCore 0:
  138.8 104.9 all-gather.1
  284.5 124.8 reduce-scatter.1
where the time goes:
time: 541 us; the launch traced here: 540 us
  waiting for transfers between devices  323 us (60%)
  blocking collectives  100 us (18%)
  local copies, waits for them, and re-layouts  41.1 us (8%)
  matrix products  40.5 us (7%)
  other arithmetic  16 us (3%)
  between operations  13.5 us (2%)
  starting transfers between devices  5.87 us (1%)
    reduce_scatter x1, waiting for transfers between devices, local(): lax.psum_scatter(partial_value.astype(jnp.bfloat16), 'width', scatter_dim...  125 us
    all_gather x1, waiting for transfers between devices, local(): arrived = lax.all_gather(arrived_cols, 'width', axis=3, tiled=True)  105 us
    all_to_all x1, blocking collectives, local(): lax.all_to_all(own_cols, 'expert', split_axis=0, concat_axis=0, tiled=True)  100 us
    all_to_all x1, waiting for transfers between devices, local(): lax.all_to_all(reduced.astype(jnp.bfloat16), 'expert', split_axis=0, conc...  93 us
    dot_general x1, matrix products, local(): jnp.einsum('skmf,kfd->skmd', hidden, down_weight, preferred_element_type=...  15.2 us
    gather x1, local copies, waits for them, and re-layouts, local(): outgoing = padded[table].reshape(n_expert, exp_local, slots, width_all)  14.3 us
    dot_general x1, matrix products, local(): jnp.einsum('skmd,kdf->skmf', arrived, up_weight, preferred_element_type=j...  14.1 us
    dot_general x1, matrix products, local(): jnp.einsum('skmd,kdf->skmf', arrived, gate_weight, preferred_element_type...  11.2 us
  transfers between devices with their start and end apart: 3, of which 3 were waited for; matrix products, arithmetic and copies ran while one was open for 0% of the time, Pallas kernels for 0%

commit v1 on v0

--- a/solution.py
+++ b/solution.py
@@ -2,6 +2,7 @@
 import jax.numpy as jnp
 from jax import lax
 from jax.sharding import PartitionSpec as P
+from jax.lax import axis_index, ppermute, psum
 
 
 def local(tokens, expert_ids, combine_weights, gate_weight, up_weight, down_weight):
@@ -26,7 +27,16 @@
     outgoing = padded[table].reshape(n_expert, exp_local, slots, width_all)
     own_cols = lax.dynamic_slice_in_dim(outgoing, lax.axis_index("width") * cols, cols, 3)
     arrived_cols = lax.all_to_all(own_cols, "expert", split_axis=0, concat_axis=0, tiled=True)
-    arrived = lax.all_gather(arrived_cols, "width", axis=3, tiled=True)
+    arr_now = psum(1, "width")
+    small = axis_index("width")
+    res, u_next = (arr_now, small)
+    arrived, m_next = (arrived_cols, 1)
+    while m_next < res:
+        t1 = ppermute(arrived, "width", [(i0, i0 ^ m_next) for i0 in range(res)])
+        y2 = jnp.concatenate([arrived, t1], axis=3)
+        piece_out = jnp.concatenate([t1, arrived], axis=3)
+        arrived = jnp.where(u_next & m_next == 0, y2, piece_out)
+        m_next = 2 * m_next
     gate = jnp.einsum("skmd,kdf->skmf", arrived, gate_weight, preferred_element_type=jnp.float32)
     up_part = jnp.einsum("skmd,kdf->skmf", arrived, up_weight, preferred_element_type=jnp.float32)
     hidden = (jax.nn.silu(gate) * up_part).astype(jnp.bfloat16)

time: 541 us -> 650 us (1.20)
  waiting for transfers between devices: 323 us -> 406 us
  other arithmetic: 16 us -> 44.7 us
    ppermute x0 -> x2, waiting for transfers between devices: none -> 189 us  [local(): t1 = ppermute(arrived, 'width', [(i0, i0 ^ m_next) for i0 in range(res)])]
    all_gather x1 -> x0, waiting for transfers between devices: 105 us -> none  [local(): arrived = lax.all_gather(arrived_cols, 'width', axis=3, tiled=True)]
    select_n x0 -> x2, other arithmetic: none -> 28.7 us  [local(): arrived = jnp.where(u_next & m_next == 0, y2, piece_out)]
  transfers between devices with their start and end apart: 3 -> 4, of which waited for: 3 -> 4; matrix products, arithmetic and copies ran while one was open for 0% -> 0% of each run, Pallas kernels for 0% -> 0%
where the time goes in v1:
time: 650 us; the launch traced here: 649 us
  waiting for transfers between devices  406 us (62%)
  blocking collectives  100 us (15%)
  other arithmetic  44.7 us (7%)
  matrix products  39.1 us (6%)
  local copies, waits for them, and re-layouts  38.7 us (6%)
  between operations  13.5 us (2%)
  starting transfers between devices  7.03 us (1%)
    ppermute x2, waiting for transfers between devices, local(): t1 = ppermute(arrived, 'width', [(i0, i0 ^ m_next) for i0 in range(res)])  189 us
    reduce_scatter x1, waiting for transfers between devices, local(): lax.psum_scatter(partial_value.astype(jnp.bfloat16), 'width', scatter_dim...  124 us
    all_to_all x1, blocking collectives, local(): lax.all_to_all(own_cols, 'expert', split_axis=0, concat_axis=0, tiled=True)  100 us
    all_to_all x1, waiting for transfers between devices, local(): lax.all_to_all(reduced.astype(jnp.bfloat16), 'expert', split_axis=0, conc...  93 us
    select_n x2, other arithmetic, local(): arrived = jnp.where(u_next & m_next == 0, y2, piece_out)  28.7 us
    dot_general x1, matrix products, local(): jnp.einsum('skmf,kfd->skmd', hidden, down_weight, preferred_element_type=...  14.6 us
    gather x1, local copies, waits for them, and re-layouts, local(): outgoing = padded[table].reshape(n_expert, exp_local, slots, width_all)  14.3 us
  transfers between devices with their start and end apart: 4, of which 4 were waited for; matrix products, arithmetic and copies ran while one was open for 0% of the time, Pallas kernels for 0%

profile of v1, /device:TPU:0, one launch (start us, length us, event | category | flops | bytes accessed | tf_op | source)
XLA Modules:
  0.0 649.3 jit_solution(18395031242053062087)
XLA Ops:
  6.5 0.0 reduce-scatter.2.cloned.1.call-start
  6.5 0.8 copy.21
  7.3 0.1 eq.37
  7.4 0.1 eq.33
  7.5 0.7 broadcast_multiply_fusion
  8.2 4.5 reduce-window.6
  12.7 0.1 slice.12
  12.8 0.1 copy.23
  13.0 0.1 copy.24
  13.1 0.1 broadcast_add_fusion
  13.2 0.1 copy.20
  13.3 0.1 mul.40
  13.4 4.3 scatter_custom_fusion
  17.7 1.3 concatenate.15
  19.1 14.3 %gather_fusion = bf16[2048,4096]{1,0:T(8,128)(2,1)} fusion(bf16[129,4096]{1,0:T(8,128)(2,1)S(1)} %concatenate.15, s32[2048]{0:T(1024)S(1)} %fusion.19), kind=kCustom, calls=%fused_computation | custom fusion | bytes 33562624 | tf_op jit(solution)/shard_map/gather | solution.py:27
  33.4 2.6 constant_dynamic-slice_fusion
  36.0 100.4 %all_to_all.10 = bf16[8,2,128,1024]{3,2,1,0:T(8,128)(2,1)} all-to-all(bf16[8,2,128,1024]{3,2,1,0:T(8,128)(2,1)S(1)} %constant_dynamic-slice_fusion), channel_id=1, replica_groups=mesh['expert'=8,'width'=4] {'expert'}, dimensions={0} | all-to-all | bytes 8388608 | tf_op jit(solution)/shard_map/all_to_all | solution.py:29
  136.4 0.0 collective-permute-start
  136.4 7.5 %collective-permute-done = bf16[8,2,128,1024]{3,2,1,0:T(8,128)(2,1)} collective-permute-done((bf16[8,2,128,1024]{3,2,1,0:T(8,128)(2,1)}, bf16[8,2,128,1024]{3,2,1,0:T(8,128)(2,1)}, u32[]{:S(2)}, u32[]{:S(2)}) %collective-permute-start) | collective-permute-done | bytes 4194336 | tf_op jit(solution)/shard_map/ppermute | solution.py:35
  143.9 11.2 %maximum_select_fusion.1 = bf16[8,2,128,2048]{3,2,1,0:T(8,128)(2,1)} fusion(bf16[8,2,128,1024]{3,2,1,0:T(8,128)(2,1)} %collective-permute-done, bf16[8,2,128,1024]{3,2,1,0:T(8,128)(2,1)} %all_to_all.10, pred[]{:T(512)S(6)} %eq.32), kind=kLoop, calls=%fused_computation.9 | loop fusion | flops 37748736 | bytes 16777216 | tf_op jit(solution)/shard_map/jit(_where)/select_n | solution.py:38
  155.1 1.5 collective-permute-start.1
  156.7 181.3 %collective-permute-done.1 = bf16[8,2,128,2048]{3,2,1,0:T(8,128)(2,1)} collective-permute-done((bf16[8,2,128,2048]{3,2,1,0:T(8,128)(2,1)}, bf16[8,2,128,2048]{3,2,1,0:T(8,128)(2,1)}, u32[]{:S(2)}, u32[]{:S(2)}) %collective-permute-start.1) | collective-permute-done | bytes 8388640 | tf_op jit(solution)/shard_map/ppermute | solution.py:35
  337.9 17.4 %maximum_select_fusion = bf16[8,2,128,4096]{3,2,1,0:T(8,128)(2,1)S(1)} fusion(bf16[8,2,128,2048]{3,2,1,0:T(8,128)(2,1)} %collective-permute-done.1, bf16[8,2,128,2048]{3,2,1,0:T(8,128)(2,1)} %maximum_select_fusion.1, pred[]{:T(512)S(6)} %eq.31), kind=kLoop, calls=%fused_computation.3 | loop fusion | flops 75497472 | bytes 33554432 | tf_op jit(solution)/shard_map/jit(_where)/select_n | solution.py:38
  355.4 12.0 %fusion.2 = f32[2,8,128,384]{3,2,1,0:T(8,128)} fusion(bf16[8,2,128,4096]{3,2,1,0:T(8,128)(2,1)S(1)} %maximum_select_fusion, bf16[2,4096,384]{2,1,0:T(8,128)(2,1)} %param.9), kind=kOutput, calls=%fused_computation.7 | convolution fusion | flops 6442450944 | bytes 26214400 | tf_op jit(solution)/shard_map/skmd,kdf->skmf/dot_general | solution.py:40
  367.4 12.5 %fusion.8 = bf16[8,2,128,384]{3,2,0,1:T(8,128)(2,1)} fusion(f32[2,8,128,384]{3,2,1,0:T(8,128)} %fusion.2, bf16[2,4096,384]{2,1,0:T(8,128)(2,1)} %param.10, bf16[8,2,128,4096]{3,2,1,0:T(8,128)(2,1)S(1)} %maximum_select_fusion), kind=kOutput, calls=%fused_computation.17 | convolution fusion | flops 6447169536 | bytes 27787264 | tf_op jit(solution)/shard_map/skmd,kdf->skmf/dot_general | solution.py:41
  379.9 14.6 %convert_bitcast_fusion = bf16[8,2,128,4096]{3,2,0,1:T(8,128)(2,1)} fusion(bf16[8,2,128,384]{3,2,0,1:T(8,128)(2,1)} %fusion.8, bf16[2,384,4096]{2,1,0:T(8,128)(2,1)} %param.11), kind=kOutput, calls=%fused_computation.4 | convolution fusion | flops 6450839552 | bytes 24641536 | tf_op jit(solution)/shard_map/skmf,kfd->skmd/dot_general | solution.py:43
  394.5 0.0 reduce-scatter.2.cloned.1.call-update
  394.5 0.0 copy-start
  394.5 124.1 %reduce-scatter.2.cloned.1.call-done = bf16[8,2,128,1024]{3,2,0,1:T(8,128)(2,1)} async-done(((bf16[8,2,128,4096]{3,2,0,1:T(8,128)(2,1)}), bf16[8,2,128,1024]{3,2,0,1:T(8,128)(2,1)}) %reduce-scatter.2.cloned.1.call-update) | async-done | bytes 4194320 | tf_op jit(solution)/shard_map/reduce_scatter | solution.py:46
  518.6 4.7 copy.27
  523.4 5.5 all-to-all-start.1
  528.9 0.0 copy-done
  528.9 0.1 copy.19
  529.0 93.0 %all-to-all-done.1 = bf16[8,2,128,1024]{3,2,1,0:T(8,128)(2,1)} async-done(((bf16[8,2,128,1024]{3,2,1,0:T(8,128)(2,1)}), bf16[8,2,128,1024]{3,2,1,0:T(8,128)(2,1)}, u32[]{:S(2)}, u32[]{:S(2)}) %all-to-all-start.1) | async-done | bytes 4194336 | tf_op jit(solution)/shard_map/all_to_all | solution.py:49
  622.0 6.5 bitcast_convert_fusion
  628.5 9.8 %gather_fusion.1 = f32[1024,1024]{1,0:T(8,128)} fusion(f32[2048,1024]{1,0:T(8,128)} %bitcast_convert_fusion, s32[1024]{0:T(1024)S(1)} %broadcast_clamp_fusion), kind=kCustom, calls=%fused_computation.1 | custom fusion | bytes 8392704 | tf_op jit(solution)/shard_map/gather | solution.py:52
  638.3 4.2 fusion.7
  (9 shorter events, 0.1 us)
Async XLA Ops:
  6.5 512.1 %reduce-scatter.2.cloned.1.call-start = ((), (), s32[]{:S(2)}) async-start(), calls=%async_computation.3 | async-start | bytes 20971520 | tf_op jit(solution)/shard_map/reduce_scatter | solution.py:46
  136.4 7.5 %collective-permute-start = (bf16[8,2,128,1024]{3,2,1,0:T(8,128)(2,1)}, bf16[8,2,128,1024]{3,2,1,0:T(8,128)(2,1)}, u32[]{:S(2)}, u32[]{:S(2)}) collective-permute-start(bf16[8,2,128,1024]{3,2,1,0:T(8,128)(2,1)} %all_to_all.10), channel_id=1, source_target_pairs={{0,1},{1,0},{2,3},{3,2},{4,5},{5,4},{6,7},{7,6},{8,9},{9,8},{10,11... | collective-permute-start | bytes 12582920 | tf_op jit(solution)/shard_map/ppermute | solution.py:35
  155.1 182.8 %collective-permute-start.1 = (bf16[8,2,128,2048]{3,2,1,0:T(8,128)(2,1)}, bf16[8,2,128,2048]{3,2,1,0:T(8,128)(2,1)}, u32[]{:S(2)}, u32[]{:S(2)}) collective-permute-start(bf16[8,2,128,2048]{3,2,1,0:T(8,128)(2,1)} %maximum_select_fusion.1), channel_id=1, source_target_pairs={{0,2},{1,3},{2,0},{3,1},{4,6},{5,7},{6,4},{7,5},{8,10},{9,11},{10,... | collective-permute-start | bytes 25165832 | tf_op jit(solution)/shard_map/ppermute | solution.py:35
  394.5 134.4 %copy-start = (f32[128,8]{0,1:T(8,128)S(1)}, f32[128,8]{0,1:T(8,128)}, u32[]{:S(2)}) copy-start(f32[128,8]{0,1:T(8,128)} %param.8) | copy-start | bytes 12292
  523.4 98.6 %all-to-all-start.1 = ((bf16[8,2,128,1024]{3,2,1,0:T(8,128)(2,1)}), bf16[8,2,128,1024]{3,2,1,0:T(8,128)(2,1)}, u32[]{:S(2)}, u32[]{:S(2)}) async-start(bf16[8,2,128,1024]{3,2,1,0:T(8,128)(2,1)} %copy.27), calls=%async_computation.2 | async-start | bytes 8388608 | tf_op jit(solution)/shard_map/all_to_all | solution.py:49
Sparse Core Ops, SparseCore 0:
  394.6 123.9 reduce-scatter.1
